TPU v7x, 32 devices: a whole 2x2x4 slice. The times are simulated.
32 devices in a mesh: dp: 8 (over z, y), tensor: 4 (over x, core).
Axes of the slice: x: 2, y: 2, z: 4, core: 2. Of those that a mesh axis runs over, the one named last changes fastest.
Arguments:
- tokens: float32 [4096, 1152], P(('dp', 'tensor')), may hold values from -6 to 6
- timesteps: int32 [16], replicated, may hold values from 0 to 999
- labels: int32 [16], replicated, may hold values from 0 to 1000
- time_weight: float32 [256, 1152], P(None, 'dp'), may hold values from -0.5 to 0.5
- class_table: float32 [1001, 1152], P(None, 'dp'), may hold values from -6 to 6
- mod_weight: bfloat16 [1, 1152, 6912], P(None, 'dp', 'tensor'), may hold values from -0.1875 to 0.1875
- mod_bias: float32 [1, 6912], replicated, may hold values from -3 to 3
- qkv_weight: bfloat16 [1, 3, 1152, 1152], P(None, None, 'dp', 'tensor'), may hold values from -0.1875 to 0.1875
- qv_bias: float32 [1, 2, 1152], replicated, may hold values from -3 to 3
- proj_weight: bfloat16 [1, 1152, 1152], P(None, 'tensor', 'dp'), may hold values from -1.25 to 1.25
- proj_bias: float32 [1, 1152], replicated, may hold values from -3 to 3
- up_weight: bfloat16 [1, 1152, 4608], P(None, 'dp', 'tensor'), may hold values from -0.1875 to 0.1875
- up_bias: float32 [1, 4608], replicated, may hold values from -3 to 3
- down_weight: bfloat16 [1, 4608, 1152], P(None, 'tensor', 'dp'), may hold values from -0.125 to 0.125
- down_bias: float32 [1, 1152], replicated, may hold values from -3 to 3
- grad_output: float32 [4096, 1152], P(('dp', 'tensor')), may hold values from -6 to 6
Outputs:
- output: float32 [4096, 1152], P(('dp', 'tensor'))
- grad_tokens: float32 [4096, 1152], P(('dp', 'tensor'))
- grad_time_weight: float32 [256, 1152], P(None, 'dp')
- grad_class_table: float32 [1001, 1152], P(None, 'dp')
- grad_mod_weight: float32 [1, 1152, 6912], P(None, 'dp', 'tensor')
- grad_mod_bias: float32 [1, 6912], replicated
- grad_qkv_weight: float32 [1, 3, 1152, 1152], P(None, None, 'dp', 'tensor')
- grad_qv_bias: float32 [1, 2, 1152], replicated
- grad_proj_weight: float32 [1, 1152, 1152], P(None, 'tensor', 'dp')
- grad_proj_bias: float32 [1, 1152], replicated
- grad_up_weight: float32 [1, 1152, 4608], P(None, 'dp', 'tensor')
- grad_up_bias: float32 [1, 4608], replicated
- grad_down_weight: float32 [1, 4608, 1152], P(None, 'tensor', 'dp')
- grad_down_bias: float32 [1, 1152], replicated
All inputs are finite; a program needn't handle non-finite values.
Results may differ from a plain program's by a relative error of at most 0.025.
Values may be sent and summed in bfloat16 or wider, within the bound.
A program may use at most 128 MiB of HBM per device.

v0:
```python
import math

import jax
import jax.numpy as jnp
from jax import lax
from jax.sharding import PartitionSpec as P

HEAD_DIM = 72
SEQ = 256
LAYERS = 1


EPSILON = 1e-06
PRECISE = lax.Precision.HIGHEST
GELU_COEFF = math.sqrt(2.0 / math.pi)
CUBIC_COEFF = 0.044715


def time_features(timesteps, width):
    half_width = width // 2
    freq_rates = jnp.exp(
        -math.log(10000.0) * jnp.arange(half_width, dtype=jnp.float32) / half_width
    )
    angles = timesteps.astype(jnp.float32)[:, None] * freq_rates[None, :]
    return jnp.concatenate([jnp.cos(angles), jnp.sin(angles)], axis=1)


def layer_norm(values):
    average = jnp.mean(values, axis=-1, keepdims=True)
    centred = values - average
    inverse = lax.rsqrt(jnp.mean(centred * centred, axis=-1, keepdims=True) + EPSILON)
    return (centred * inverse, inverse)


def norm_back(normed, inverse, grad_normed):
    first = jnp.mean(grad_normed, axis=-1, keepdims=True)
    second = jnp.mean(grad_normed * normed, axis=-1, keepdims=True)
    return inverse * (grad_normed - first - normed * second)


def gelu_value(values):
    return (
        0.5
        * values
        * (1.0 + jnp.tanh(GELU_COEFF * (values + CUBIC_COEFF * values * values * values)))
    )


def gelu_slope(values):
    tangent = jnp.tanh(GELU_COEFF * (values + CUBIC_COEFF * values * values * values))
    return 0.5 * (1.0 + tangent) + 0.5 * values * (1.0 - tangent * tangent) * GELU_COEFF * (
        1.0 + 3.0 * CUBIC_COEFF * values * values
    )


def silu_slope(values):
    logistic = jax.nn.sigmoid(values)
    return logistic * (1.0 + values * (1.0 - logistic))


def split_heads(values, latent_count):
    return values.reshape(latent_count, SEQ, -1, HEAD_DIM)


def local(
    tokens,
    timesteps,
    labels,
    time_weight,
    class_table,
    mod_weight,
    mod_bias,
    qkv_weight,
    qv_bias,
    proj_weight,
    proj_bias,
    up_weight,
    up_bias,
    down_weight,
    down_bias,
    grad_output,
):
    rows_own, model_width = tokens.shape
    tensor_count = lax.axis_size("tensor")
    tensor_place = lax.axis_index("tensor")
    group_rows = rows_own * tensor_count
    latent_count = group_rows // SEQ
    head_cols = qkv_weight.shape[3]
    unit_cols = up_weight.shape[2]
    mod_cols = mod_weight.shape[2]
    head_start = tensor_place * head_cols
    unit_start = tensor_place * unit_cols
    col_start = tensor_place * mod_cols
    score_scale = 1.0 / math.sqrt(HEAD_DIM)
    features = time_features(timesteps, time_weight.shape[0])
    one_hot = (
        labels[:, None] == jnp.arange(class_table.shape[0], dtype=jnp.int32)[None, :]
    ).astype(jnp.float32)
    condition = jnp.dot(features, time_weight, precision=PRECISE) + jnp.dot(
        one_hot, class_table, precision=PRECISE
    )
    cond_act = jax.nn.silu(condition).astype(jnp.bfloat16)
    mod_terms = jnp.stack([jnp.dot(cond_act, mod_weight[0], preferred_element_type=jnp.float32)])
    mod_own = lax.psum_scatter(mod_terms, "dp", scatter_dimension=1, tiled=True)
    mod_own = mod_own + lax.dynamic_slice_in_dim(mod_bias, col_start, mod_cols, 1)[:, None, :]
    modulation = lax.all_gather(mod_own, "tensor", axis=2, tiled=True)
    row_latent = (tensor_place * rows_own + jnp.arange(rows_own, dtype=jnp.int32)) // SEQ
    selector = (row_latent[:, None] == jnp.arange(latent_count, dtype=jnp.int32)[None, :]).astype(
        jnp.float32
    )

    def per_row(values):
        return jnp.dot(selector, values, precision=PRECISE)

    def per_latent(values):
        return jnp.dot(selector.T, values, precision=PRECISE)

    def mod_pieces(current):
        rows_mod = per_row(modulation[current])
        return [
            rows_mod[:, segment * model_width : (segment + 1) * model_width] for segment in range(6)
        ]

    def gather_layer(current):
        return (
            lax.all_gather(qkv_weight[current], "dp", axis=1, tiled=True),
            lax.all_gather(proj_weight[current], "dp", axis=1, tiled=True),
            lax.all_gather(up_weight[current], "dp", axis=0, tiled=True),
            lax.all_gather(down_weight[current], "dp", axis=1, tiled=True),
        )

    def spread_rows(values):
        return lax.all_gather(values, "tensor", axis=0, tiled=True)

    def sum_rows(values):
        return lax.psum_scatter(
            values.astype(jnp.bfloat16), "tensor", scatter_dimension=0, tiled=True
        ).astype(jnp.float32)

    def spread_grads(values):
        return lax.all_gather(values, "tensor", axis=0, tiled=True)

    def sum_grads(values):
        return lax.psum_scatter(
            values.astype(jnp.bfloat16), "tensor", scatter_dimension=0, tiled=True
        ).astype(jnp.float32)

    def attention_scores(queries, key_rows):
        return (
            jnp.einsum(
                "bqhd,bkhd->bhqk",
                split_heads(queries, latent_count),
                split_heads(key_rows, latent_count),
                preferred_element_type=jnp.float32,
            )
            * score_scale
        )

    kept_weights = []
    current_x = tokens
    current = 0
    layer_full = gather_layer(current)
    kept_weights.append(layer_full)
    qkv_full, proj_full, up_full, down_full = layer_full
    shift_attn, scale_attn, gate_attn, shift_mlp, scale_mlp, gate_mlp = mod_pieces(current)
    bias_query = lax.dynamic_slice_in_dim(qv_bias[current, 0], head_start, head_cols, 0)
    bias_value = lax.dynamic_slice_in_dim(qv_bias[current, 1], head_start, head_cols, 0)
    unit_bias = lax.dynamic_slice_in_dim(up_bias[current], unit_start, unit_cols, 0)
    normed_attn, inverse_attn = layer_norm(current_x)
    attn_in = spread_rows((normed_attn * (1.0 + scale_attn) + shift_attn).astype(jnp.bfloat16))
    queries = (
        jnp.dot(attn_in, qkv_full[0], preferred_element_type=jnp.float32) + bias_query
    ).astype(jnp.bfloat16)
    key_rows = jnp.dot(attn_in, qkv_full[1], preferred_element_type=jnp.float32).astype(
        jnp.bfloat16
    )
    value_rows = (
        jnp.dot(attn_in, qkv_full[2], preferred_element_type=jnp.float32) + bias_value
    ).astype(jnp.bfloat16)
    scores = attention_scores(queries, key_rows)
    log_total = jnp.log(jnp.sum(jnp.exp(scores), axis=-1, keepdims=True))
    prob_low = jnp.exp(scores - log_total).astype(jnp.bfloat16)
    attended = (
        jnp.einsum(
            "bhqk,bkhd->bqhd",
            prob_low,
            split_heads(value_rows, latent_count),
            preferred_element_type=jnp.float32,
        )
        .astype(jnp.bfloat16)
        .reshape(group_rows, head_cols)
    )
    attn_out = (
        sum_rows(jnp.dot(attended, proj_full, preferred_element_type=jnp.float32))
        + proj_bias[current]
    )
    middle = current_x + gate_attn * attn_out
    normed_mlp, inverse_mlp = layer_norm(middle)
    mlp_in = spread_rows((normed_mlp * (1.0 + scale_mlp) + shift_mlp).astype(jnp.bfloat16))
    pre_act = jnp.dot(mlp_in, up_full, preferred_element_type=jnp.float32) + unit_bias
    gelu_low = gelu_value(pre_act).astype(jnp.bfloat16)
    mlp_out = (
        sum_rows(jnp.dot(gelu_low, down_full, preferred_element_type=jnp.float32))
        + down_bias[current]
    )
    stored = [
        (
            normed_attn,
            inverse_attn,
            attn_in,
            queries,
            key_rows,
            value_rows,
            log_total,
            attended,
            attn_out,
            normed_mlp,
            inverse_mlp,
            mlp_in,
            pre_act,
            gelu_low,
            mlp_out,
        )
    ]
    current_x = middle + gate_mlp * mlp_out
    grad_x = grad_output
    mod_list = [None] * LAYERS
    qkv_list = [None] * LAYERS
    proj_list = [None] * LAYERS
    up_list = [None] * LAYERS
    down_list = [None] * LAYERS
    qv_bias_list = [None] * LAYERS
    proj_bias_list = [None] * LAYERS
    unit_bias_list = [None] * LAYERS
    down_bias_list = [None] * LAYERS
    for current in reversed(range(LAYERS)):
        (
            normed_attn,
            inverse_attn,
            attn_in,
            queries,
            key_rows,
            value_rows,
            log_total,
            attended,
            attn_out,
            normed_mlp,
            inverse_mlp,
            mlp_in,
            pre_act,
            gelu_low,
            mlp_out,
        ) = stored[current]
        qkv_full, proj_full, up_full, down_full = gather_layer(current)
        shift_attn, scale_attn, gate_attn, shift_mlp, scale_mlp, gate_mlp = mod_pieces(current)
        d_mlp = grad_x * gate_mlp
        d_gate_mlp = per_latent(grad_x * mlp_out)
        down_bias_list[current] = jnp.sum(d_mlp, axis=0)
        d_mlp_all = spread_grads(d_mlp.astype(jnp.bfloat16))
        grad_down = jnp.dot(gelu_low.T, d_mlp_all, preferred_element_type=jnp.float32)
        d_gelu = jnp.dot(d_mlp_all, down_full.T, preferred_element_type=jnp.float32)
        d_pre = d_gelu * gelu_slope(pre_act)
        unit_part = jnp.sum(d_pre, axis=0)
        unit_bias_list[current] = lax.dynamic_update_slice_in_dim(
            jnp.zeros((up_bias.shape[1],), jnp.float32), unit_part, unit_start, 0
        )
        d_pre_low = d_pre.astype(jnp.bfloat16)
        grad_up = jnp.dot(mlp_in.T, d_pre_low, preferred_element_type=jnp.float32)
        d_mlp_in = sum_grads(jnp.dot(d_pre_low, up_full.T, preferred_element_type=jnp.float32))
        d_shift_mlp = per_latent(d_mlp_in)
        d_scale_mlp = per_latent(d_mlp_in * normed_mlp)
        d_middle = grad_x + norm_back(normed_mlp, inverse_mlp, d_mlp_in * (1.0 + scale_mlp))
        d_attn = d_middle * gate_attn
        d_gate_attn = per_latent(d_middle * attn_out)
        proj_bias_list[current] = jnp.sum(d_attn, axis=0)
        d_attn_all = spread_grads(d_attn.astype(jnp.bfloat16))
        grad_proj = jnp.dot(attended.T, d_attn_all, preferred_element_type=jnp.float32)
        d_attended = jnp.dot(d_attn_all, proj_full.T, preferred_element_type=jnp.float32).astype(
            jnp.bfloat16
        )
        scores = attention_scores(queries, key_rows)
        prob_full = jnp.exp(scores - log_total)
        prob_low = prob_full.astype(jnp.bfloat16)
        d_heads = split_heads(d_attended, latent_count)
        grad_value = jnp.einsum(
            "bhqk,bqhd->bkhd", prob_low, d_heads, preferred_element_type=jnp.float32
        ).reshape(group_rows, head_cols)
        d_prob = jnp.einsum(
            "bqhd,bkhd->bhqk",
            d_heads,
            split_heads(value_rows, latent_count),
            preferred_element_type=jnp.float32,
        )
        row_delta = jnp.einsum(
            "bqhd,bqhd->bhq",
            d_heads,
            split_heads(attended, latent_count),
            preferred_element_type=jnp.float32,
        )
        d_scores = prob_full * (d_prob - row_delta[..., None])
        d_score_low = d_scores.astype(jnp.bfloat16)
        grad_query = (
            jnp.einsum(
                "bhqk,bkhd->bqhd",
                d_score_low,
                split_heads(key_rows, latent_count),
                preferred_element_type=jnp.float32,
            ).reshape(group_rows, head_cols)
            * score_scale
        )
        grad_key = (
            jnp.einsum(
                "bhqk,bqhd->bkhd",
                d_score_low,
                split_heads(queries, latent_count),
                preferred_element_type=jnp.float32,
            ).reshape(group_rows, head_cols)
            * score_scale
        )
        qv_part = jnp.stack([jnp.sum(grad_query, axis=0), jnp.sum(grad_value, axis=0)])
        qv_bias_list[current] = lax.dynamic_update_slice_in_dim(
            jnp.zeros((2, model_width), jnp.float32), qv_part, head_start, 1
        )
        query_low = grad_query.astype(jnp.bfloat16)
        key_low = grad_key.astype(jnp.bfloat16)
        value_low = grad_value.astype(jnp.bfloat16)
        grad_qkv = jnp.stack(
            [
                jnp.dot(attn_in.T, query_low, preferred_element_type=jnp.float32),
                jnp.dot(attn_in.T, key_low, preferred_element_type=jnp.float32),
                jnp.dot(attn_in.T, value_low, preferred_element_type=jnp.float32),
            ]
        )
        d_attn_terms = (
            jnp.dot(query_low, qkv_full[0].T, preferred_element_type=jnp.float32)
            + jnp.dot(key_low, qkv_full[1].T, preferred_element_type=jnp.float32)
            + jnp.dot(value_low, qkv_full[2].T, preferred_element_type=jnp.float32)
        )
        d_attn_in = sum_grads(d_attn_terms)
        d_shift_attn = per_latent(d_attn_in)
        d_scale_attn = per_latent(d_attn_in * normed_attn)
        grad_x = d_middle + norm_back(normed_attn, inverse_attn, d_attn_in * (1.0 + scale_attn))
        mod_list[current] = jnp.concatenate(
            [d_shift_attn, d_scale_attn, d_gate_attn, d_shift_mlp, d_scale_mlp, d_gate_mlp], axis=1
        )
        qkv_list[current], proj_list[current], up_list[current], down_list[current] = (
            lax.psum_scatter(
                grad_qkv.astype(jnp.bfloat16), "dp", scatter_dimension=1, tiled=True
            ).astype(jnp.float32),
            lax.psum_scatter(
                grad_proj.astype(jnp.bfloat16), "dp", scatter_dimension=1, tiled=True
            ).astype(jnp.float32),
            lax.psum_scatter(
                grad_up.astype(jnp.bfloat16), "dp", scatter_dimension=0, tiled=True
            ).astype(jnp.float32),
            lax.psum_scatter(
                grad_down.astype(jnp.bfloat16), "dp", scatter_dimension=1, tiled=True
            ).astype(jnp.float32),
        )
    d_mod_part = jnp.stack(mod_list)
    qv_total, proj_total, unit_total, down_total, modb_total = lax.psum(
        (
            jnp.stack(qv_bias_list),
            jnp.stack(proj_bias_list),
            jnp.stack(unit_bias_list),
            jnp.stack(down_bias_list),
            jnp.sum(d_mod_part, axis=1),
        ),
        ("dp", "tensor"),
    )
    d_mod = lax.psum(d_mod_part.astype(jnp.bfloat16), "tensor").astype(jnp.float32)
    d_mod_all = lax.all_gather(
        lax.dynamic_slice_in_dim(d_mod, col_start, mod_cols, 2), "dp", axis=1, tiled=True
    )
    cond_wide = cond_act.astype(jnp.float32)
    grad_mod_weight = jnp.stack([jnp.dot(cond_wide.T, d_mod_all[0], precision=PRECISE)])
    cond_back = jnp.dot(d_mod_all[0], mod_weight[0].astype(jnp.float32).T, precision=PRECISE)
    d_cond_act = lax.psum(cond_back, "tensor")
    d_condition = d_cond_act * silu_slope(condition)
    grad_time_weight = jnp.dot(features.T, d_condition, precision=PRECISE)
    grad_class_table = jnp.dot(one_hot.T, d_condition, precision=PRECISE)
    return (
        current_x,
        grad_x,
        grad_time_weight,
        grad_class_table,
        grad_mod_weight,
        modb_total,
        jnp.stack(qkv_list),
        qv_total,
        jnp.stack(proj_list),
        proj_total,
        jnp.stack(up_list),
        unit_total,
        jnp.stack(down_list),
        down_total,
    )


def solution(mesh):
    in_specs = (
        P(("dp", "tensor"), None),
        P(),
        P(),
        P(None, "dp"),
        P(None, "dp"),
        P(None, "dp", "tensor"),
        P(),
        P(None, None, "dp", "tensor"),
        P(),
        P(None, "tensor", "dp"),
        P(),
        P(None, "dp", "tensor"),
        P(),
        P(None, "tensor", "dp"),
        P(),
        P(("dp", "tensor"), None),
    )
    out_specs = (
        P(("dp", "tensor"), None),
        P(("dp", "tensor"), None),
        P(None, "dp"),
        P(None, "dp"),
        P(None, "dp", "tensor"),
        P(),
        P(None, None, "dp", "tensor"),
        P(),
        P(None, "tensor", "dp"),
        P(),
        P(None, "dp", "tensor"),
        P(),
        P(None, "tensor", "dp"),
        P(),
    )
    return jax.shard_map(local, mesh=mesh, in_specs=in_specs, out_specs=out_specs, check_vma=False)
```

profile of v0, /device:TPU:0, one launch (start us, length us, event | category | flops | bytes accessed | tf_op | source)
XLA Modules:
  0.0 829.2 jit_solution(17721218927461385044)
XLA Ops:
  16.1 69.0 %all-reduce.4.cloned.1.call-done = f32[1,16,1728]{2,1,0:T(8,128)} async-done(((f32[1,16,1728]{2,1,0:T(8,128)}), f32[1,16,1728]{2,1,0:T(8,128)}) %all-reduce.4.cloned.1.call-update) | async-done | bytes 110608
  87.2 23.5 %all_gather.34 = f32[1,2,6912]{1,0,2:T(1,128)S(1)} all-gather(f32[1,2,1728]{1,0,2:T(1,128)S(1)} %copy.63), channel_id=1, replica_groups=mesh['dp'=8,'tensor'=4] {'tensor'}, dimensions={2}, use_global_device_ids=true | all-gather | bytes 69120 | tf_op jit(solution)/shard_map/all_gather | solution.py:106
  116.6 35.3 %all-gather.1 = bf16[1,288,1152]{1,2,0:T(8,128)(2,1)} all-gather(bf16[1,288,144]{1,2,0:T(8,128)(2,1)S(1)} %copy-done.24), channel_id=3, replica_groups=mesh['dp'=8,'tensor'=4] {'dp'}, dimensions={2}, use_global_device_ids=true | all-gather | bytes 746496 | tf_op jit(solution)/shard_map/all_gather | solution.py:127
  151.9 38.0 %all-gather.20.cloned.1.call-done = bf16[1,3,1152,288]{3,2,1,0:T(8,128)(2,1)} async-done(((bf16[1,3,144,288]{3,2,1,0:T(8,128)(2,1)}), bf16[1,3,1152,288]{3,2,1,0:T(8,128)(2,1)}) %all-gather.20.cloned.1.call-update) | async-done | bytes 1990672 | tf_op jit(solution)/shard_map/all_gather | solution.py:126
  197.9 3.0 convolution_convert_fusion.11
  202.1 3.0 convolution_convert_fusion.4
  205.9 23.7 %reduce-scatter.12.cloned.1.call-done = bf16[128,1152]{1,0:T(8,128)(2,1)} async-done(((bf16[512,1152]{1,0:T(8,128)(2,1)}), bf16[128,1152]{1,0:T(8,128)(2,1)}) %reduce-scatter.12.cloned.1.call-update) | async-done | bytes 294928 | tf_op jit(solution)/shard_map/reduce_scatter | solution.py:136
  236.0 50.5 %all-gather.22.cloned.1.call-done = bf16[1,1152,1152]{2,1,0:T(8,128)(2,1)} async-done(((bf16[1,144,1152]{2,1,0:T(8,128)(2,1)}), bf16[1,1152,1152]{2,1,0:T(8,128)(2,1)}) %all-gather.22.cloned.1.call-update) | async-done | bytes 2654224 | tf_op jit(solution)/shard_map/all_gather | solution.py:128
  286.5 18.0 %all-gather.14.cloned.1.call-done = bf16[512,1152]{1,0:T(8,128)(2,1)} async-done(((bf16[128,1152]{1,0:T(8,128)(2,1)}), bf16[512,1152]{1,0:T(8,128)(2,1)}) %all-gather.14.cloned.1.call-update) | async-done | bytes 1179664 | tf_op jit(solution)/shard_map/all_gather | solution.py:133
  304.6 5.4 convolution_add_fusion.2
  309.9 51.8 %all-gather.24.cloned.1.call-done = bf16[1,1152,1152]{1,2,0:T(8,128)(2,1)} async-done(((bf16[1,1152,144]{1,2,0:T(8,128)(2,1)}), bf16[1,1152,1152]{1,2,0:T(8,128)(2,1)}) %all-gather.24.cloned.1.call-update) | async-done | bytes 2654224 | tf_op jit(solution)/shard_map/all_gather | solution.py:129
  361.7 18.2 %all-gather.16.cloned.1.call-done = bf16[512,1152]{1,0:T(8,128)(2,1)} async-done(((bf16[128,1152]{1,0:T(8,128)(2,1)}), bf16[512,1152]{1,0:T(8,128)(2,1)}) %all-gather.16.cloned.1.call-update) | async-done | bytes 1179664 | tf_op jit(solution)/shard_map/all_gather | solution.py:141
  379.9 6.0 fusion.104
  387.0 2.9 convolution_convert_fusion.2
  389.9 5.7 convolution_convert_fusion.3
  396.4 19.3 %reduce-scatter.16.cloned.1.call-done = bf16[128,1152]{1,0:T(8,128)(2,1)} async-done(((bf16[512,1152]{1,0:T(8,128)(2,1)}), bf16[128,1152]{1,0:T(8,128)(2,1)}) %reduce-scatter.16.cloned.1.call-update) | async-done | bytes 294928 | tf_op jit(solution)/shard_map/reduce_scatter | solution.py:144
  418.1 25.6 %reduce-scatter.14.cloned.1.call-done = bf16[128,1152]{1,0:T(8,128)(2,1)} async-done(((bf16[512,1152]{1,0:T(8,128)(2,1)}), bf16[128,1152]{1,0:T(8,128)(2,1)}) %reduce-scatter.14.cloned.1.call-update) | async-done | bytes 294928 | tf_op jit(solution)/shard_map/reduce_scatter | solution.py:136
  446.5 4.9 convolution_convert_fusion.1
  451.5 5.4 convolution_convert_fusion
  457.2 4.2 fusion.14
  464.1 2.8 convolution_convert_fusion.9
  477.9 4.5 fusion.100
  498.5 7.2 copy.97
  505.7 7.5 reshape.264
  513.6 25.3 %reduce-scatter.22.cloned.1.call-done = bf16[144,1152]{1,0:T(8,128)(2,1)} async-done(((bf16[1152,1152]{1,0:T(8,128)(2,1)}), bf16[144,1152]{1,0:T(8,128)(2,1)}) %reduce-scatter.22.cloned.1.call-update) | async-done | bytes 331792 | tf_op jit(solution)/shard_map/reduce_scatter | solution.py:353
  540.8 72.5 %reduce-scatter.24.cloned.1.call-done = bf16[1152,144]{0,1:T(8,128)(2,1)} async-done(((bf16[1152,1152]{0,1:T(8,128)(2,1)}), bf16[1152,144]{0,1:T(8,128)(2,1)}) %reduce-scatter.24.cloned.1.call-update) | async-done | bytes 331792 | tf_op jit(solution)/shard_map/reduce_scatter | solution.py:356
  615.2 63.2 %reduce-scatter.20.cloned.1.call-done = bf16[288,144]{0,1:T(8,128)(2,1)} async-done(((bf16[288,1152]{0,1:T(8,128)(2,1)}), bf16[288,144]{0,1:T(8,128)(2,1)}) %reduce-scatter.20.cloned.1.call-update) | async-done | bytes 82960 | tf_op jit(solution)/shard_map/reduce_scatter | solution.py:350
  679.9 25.2 %reduce-scatter.18.cloned.1.call-done = bf16[128,1152]{1,0:T(8,128)(2,1)} async-done(((bf16[512,1152]{1,0:T(8,128)(2,1)}), bf16[128,1152]{1,0:T(8,128)(2,1)}) %reduce-scatter.18.cloned.1.call-update) | async-done | bytes 294928 | tf_op jit(solution)/shard_map/reduce_scatter | solution.py:144
  719.3 10.7 %psum.49 = bf16[1,2,6912]{2,1,0:T(2,128)(2,1)S(1)} all-reduce(bf16[1,2,6912]{2,1,0:T(2,128)(2,1)S(1)} %copy-done.35), channel_id=1, replica_groups=mesh['dp'=8,'tensor'=4] {'tensor'}, use_global_device_ids=true, to_apply=%region_14.15 | all-reduce | flops 13824 | bytes 55296 | tf_op jit(solution)/shard_map/psum | solution.py:371
  730.1 31.1 %all_gather.43 = f32[1,16,1728]{2,0,1:T(1,128)S(1)} all-gather(f32[1,2,1728]{2,0,1:T(1,128)S(1)} %copy.81), channel_id=1, replica_groups=mesh['dp'=8,'tensor'=4] {'dp'}, dimensions={1}, use_global_device_ids=true | all-gather | bytes 124416 | tf_op jit(solution)/shard_map/all_gather | solution.py:372
  761.7 11.0 %psum.50 = f32[16,144]{1,0:T(8,128)S(1)} all-reduce(f32[16,144]{1,0:T(8,128)S(1)} %fusion.39), channel_id=1, replica_groups=mesh['dp'=8,'tensor'=4] {'tensor'}, use_global_device_ids=true, to_apply=%region_15.16 | all-reduce | flops 2304 | bytes 18432 | tf_op jit(solution)/shard_map/psum | solution.py:378
  772.7 40.3 %all-reduce.1 = (f32[1,6912]{1,0:T(1,128)}, f32[1,2,1152]{2,1,0:T(2,128)}, f32[1,1152]{1,0:T(1,128)}, f32[1,4608]{1,0:T(1,128)}, f32[1,1152]{1,0:T(1,128)}) all-reduce(f32[1,6912]{1,0:T(1,128)S(1)} %reduce_sum.147, f32[1,2,1152]{2,1,0:T(2,128)S(1)} %copy-done.33, ...), channel_id=1, replica_groups=mesh['dp'=8,'tensor'=4] {'dp','tensor'}, use_global_device_ids=true, to_apply=%region_17.18 | all-reduce | flops 16128 | bytes 129024 | tf_op jit(solution)/shard_map/psum | solution.py:361
  (242 shorter events, 98.4 us)
Async XLA Ops:
  7.2 77.9 %all-reduce.4.cloned.1.call-start = ((), (), s32[]{:S(2)}) async-start(), calls=%async_computation.23 | async-start | bytes 229376
  8.4 76.7 %copy-start.26 = (f32[16,128]{1,0:T(8,128)}, f32[16,128]{1,0:T(8,128)S(1)}, u32[]{:S(2)}) copy-start(f32[16,128]{1,0:T(8,128)S(1)} %get-tuple-element.82) | copy-start | bytes 24580
  8.4 76.7 %copy-start.28 = (f32[16,128]{1,0:T(8,128)}, f32[16,128]{1,0:T(8,128)S(1)}, u32[]{:S(2)}) copy-start(f32[16,128]{1,0:T(8,128)S(1)} %get-tuple-element.83) | copy-start | bytes 24580
  12.6 139.3 %all-gather.12.cloned.1.call-start = ((), (), s32[]{:S(2)}) async-start(), calls=%async_computation.8 | async-start | bytes 1474560 | tf_op jit(solution)/shard_map/all_gather | solution.py:133
  13.8 99.2 %copy-start.37 = (f32[128]{0:T(128)}, f32[128]{0:T(128)S(1)}, u32[]{:S(2)}) copy-start(f32[128]{0:T(128)S(1)} %broadcast_multiply_fusion.5) | copy-start | bytes 1540
  14.0 99.0 %copy-start.41 = (f32[128]{0:T(128)}, f32[128]{0:T(128)S(1)}, u32[]{:S(2)}) copy-start(f32[128]{0:T(128)S(1)} %add_rsqrt_fusion.1) | copy-start | bytes 1540
  16.1 94.6 %copy-start.36 = (s32[128]{0:T(128)}, s32[128]{0:T(128)S(1)}, u32[]{:S(2)}) copy-start(s32[128]{0:T(128)S(1)} %and_select_fusion) | copy-start | bytes 1540
  115.7 74.2 %all-gather.20.cloned.1.call-start = ((), (), s32[]{:S(2)}) async-start(), calls=%async_computation.19 | async-start | bytes 2985984 | tf_op jit(solution)/shard_map/all_gather | solution.py:126
  116.5 113.1 %reduce-scatter.12.cloned.1.call-start = ((), (), s32[]{:S(2)}) async-start(), calls=%async_computation.9 | async-start | bytes 1474560 | tf_op jit(solution)/shard_map/reduce_scatter | solution.py:136
  205.2 81.4 %all-gather.22.cloned.1.call-start = ((), (), s32[]{:S(2)}) async-start(), calls=%async_computation.20 | async-start | bytes 2985984 | tf_op jit(solution)/shard_map/all_gather | solution.py:128
  205.8 98.8 %all-gather.14.cloned.1.call-start = ((), (), s32[]{:S(2)}) async-start(), calls=%async_computation.10 | async-start | bytes 1474560 | tf_op jit(solution)/shard_map/all_gather | solution.py:133
  230.9 184.8 %copy-start.39 = (f32[128]{0:T(128)}, f32[128]{0:T(128)S(1)}, u32[]{:S(2)}) copy-start(f32[128]{0:T(128)S(1)} %broadcast_multiply_fusion.4) | copy-start | bytes 1540
  231.1 184.6 %copy-start.43 = (f32[128]{0:T(128)}, f32[128]{0:T(128)S(1)}, u32[]{:S(2)}) copy-start(f32[128]{0:T(128)S(1)} %add_rsqrt_fusion) | copy-start | bytes 1540
  233.6 128.2 %all-gather.24.cloned.1.call-start = ((), (), s32[]{:S(2)}) async-start(), calls=%async_computation.21 | async-start | bytes 2985984 | tf_op jit(solution)/shard_map/all_gather | solution.py:129
  234.3 145.6 %all-gather.16.cloned.1.call-start = ((), (), s32[]{:S(2)}) async-start(), calls=%async_computation.12 | async-start | bytes 1474560 | tf_op jit(solution)/shard_map/all_gather | solution.py:141
  235.1 180.6 %reduce-scatter.16.cloned.1.call-start = ((), (), s32[]{:S(2)}) async-start(), calls=%async_computation.13 | async-start | bytes 1474560 | tf_op jit(solution)/shard_map/reduce_scatter | solution.py:144
  389.9 53.8 %reduce-scatter.14.cloned.1.call-start = ((), (), s32[]{:S(2)}) async-start(), calls=%async_computation.11 | async-start | bytes 1474560 | tf_op jit(solution)/shard_map/reduce_scatter | solution.py:136
  395.7 68.4 %all-gather.18.cloned.1.call-start = ((), (), s32[]{:S(2)}) async-start(), calls=%async_computation.14 | async-start | bytes 1474560 | tf_op jit(solution)/shard_map/all_gather | solution.py:141
  446.5 92.5 %reduce-scatter.22.cloned.1.call-start = ((), (), s32[]{:S(2)}) async-start(), calls=%async_computation.17 | async-start | bytes 2985984 | tf_op jit(solution)/shard_map/reduce_scatter | solution.py:353
  451.5 161.9 %reduce-scatter.24.cloned.1.call-start = ((), (), s32[]{:S(2)}) async-start(), calls=%async_computation.18 | async-start | bytes 2985984 | tf_op jit(solution)/shard_map/reduce_scatter | solution.py:356
  457.0 221.4 %reduce-scatter.20.cloned.1.call-start = ((), (), s32[]{:S(2)}) async-start(), calls=%async_computation.16 | async-start | bytes 995328 | tf_op jit(solution)/shard_map/reduce_scatter | solution.py:350
  477.8 227.3 %reduce-scatter.18.cloned.1.call-start = ((), (), s32[]{:S(2)}) async-start(), calls=%async_computation.15 | async-start | bytes 1474560 | tf_op jit(solution)/shard_map/reduce_scatter | solution.py:144
  491.2 327.9 %reduce-scatter.26.cloned.1.call-start = ((), (), s32[]{:S(2)}) async-start(), calls=%async_computation.22 | async-start | bytes 2322432
  513.4 195.8 %copy-start.17 = (bf16[128,1152]{1,0:T(8,128)(2,1)S(1)}, bf16[128,1152]{1,0:T(8,128)(2,1)}, u32[]{:S(2)}) copy-start(bf16[128,1152]{1,0:T(8,128)(2,1)} %reduce-scatter.12.cloned.1.call-done) | copy-start | bytes 884740
  513.4 197.5 %copy-start.10 = (bf16[128,1152]{1,0:T(8,128)(2,1)S(1)}, bf16[128,1152]{1,0:T(8,128)(2,1)}, u32[]{:S(2)}) copy-start(bf16[128,1152]{1,0:T(8,128)(2,1)} %reduce-scatter.16.cloned.1.call-done) | copy-start | bytes 884740
  513.6 166.3 %copy-start.32 = (f32[1,2,1152]{2,1,0:T(2,128)}, f32[1,2,1152]{2,1,0:T(2,128)S(1)}, u32[]{:S(2)}) copy-start(f32[1,2,1152]{2,1,0:T(2,128)S(1)} %dynamic_update_slice.8) | copy-start | bytes 27652
  540.8 173.4 %copy-start.18 = (bf16[128,1152]{1,0:T(8,128)(2,1)S(1)}, bf16[128,1152]{1,0:T(8,128)(2,1)}, u32[]{:S(2)}) copy-start(bf16[128,1152]{1,0:T(8,128)(2,1)} %reduce-scatter.14.cloned.1.call-done) | copy-start | bytes 884740
  717.5 97.1 %copy-start.27 = (f32[16,128]{1,0:T(8,128)S(1)}, f32[16,128]{1,0:T(8,128)}, u32[]{:S(2)}) copy-start(f32[16,128]{1,0:T(8,128)} %copy-done.26) | copy-start | bytes 24580
  717.5 97.1 %copy-start.29 = (f32[16,128]{1,0:T(8,128)S(1)}, f32[16,128]{1,0:T(8,128)}, u32[]{:S(2)}) copy-start(f32[16,128]{1,0:T(8,128)} %copy-done.28) | copy-start | bytes 24580
  717.5 98.1 %copy-start.48 = (s32[16]{0:T(128)S(1)}, s32[16]{0:T(128)}, u32[]{:S(2)}) copy-start(s32[16]{0:T(128)} %param.18) | copy-start | bytes 196
  719.2 97.7 %copy-start.38 = (f32[128]{0:T(128)S(1)}, f32[128]{0:T(128)}, u32[]{:S(2)}) copy-start(f32[128]{0:T(128)} %copy-done.37) | copy-start | bytes 1540
  719.2 97.7 %copy-start.42 = (f32[128]{0:T(128)S(1)}, f32[128]{0:T(128)}, u32[]{:S(2)}) copy-start(f32[128]{0:T(128)} %copy-done.41) | copy-start | bytes 1540
  (36 other events, 370.7 us)
Sparse Core Ops, SparseCore 0:
  12.7 72.4 all-reduce.3
  115.8 16.3 all-gather.11
  134.5 55.3 all-gather.19
  205.3 24.1 reduce-scatter.11
  231.5 54.9 all-gather.21
  288.5 15.9 all-gather.13
  306.7 54.9 all-gather.23
  363.9 15.9 all-gather.15
  390.0 25.6 reduce-scatter.15
  418.1 25.6 reduce-scatter.13
  446.6 17.4 all-gather.17
  467.6 71.3 reduce-scatter.21
  542.6 70.6 reduce-scatter.23
  617.2 61.1 reduce-scatter.19
  680.8 24.3 reduce-scatter.17
  708.6 68.2 reduce-scatter.25
where the time goes:
time: 838 us; the launch traced here: 829 us
  waiting for transfers between devices  506 us (60%)
  blocking collectives  152 us (18%)
  matrix products  82.3 us (10%)
  local copies, waits for them, and re-layouts  39.9 us (5%)
  other arithmetic  32.1 us (4%)
  between operations  15.9 us (2%)
    reduce_scatter x1, waiting for transfers between devices, local(): lax.psum_scatter(grad_down.astype(jnp.bfloat16), 'dp', scatter_dimension=...  72.5 us
    unnamed x18, waiting for transfers between devices  71.8 us
    reduce_scatter x1, waiting for transfers between devices, local(): lax.psum_scatter(grad_proj.astype(jnp.bfloat16), 'dp', scatter_dimension=...  63.2 us
    all_gather x1, waiting for transfers between devices, gather_layer(): lax.all_gather(down_weight[current], 'dp', axis=1, tiled=True)  51.8 us
    all_gather x1, waiting for transfers between devices, gather_layer(): lax.all_gather(up_weight[current], 'dp', axis=0, tiled=True)  50.5 us
    reduce_scatter x2, waiting for transfers between devices, sum_rows(): lax.psum_scatter(values.astype(jnp.bfloat16), 'tensor', scatter_dimension...  49.3 us
    reduce_scatter x2, waiting for transfers between devices, sum_grads(): lax.psum_scatter(values.astype(jnp.bfloat16), 'tensor', scatter_dimension...  44.5 us
    psum x1, blocking collectives, local(): lax.psum((jnp.stack(qv_bias_list), jnp.stack(proj_bias_list), jnp.stack(u...  40.3 us
  transfers between devices with their start and end apart: 16, of which 14 were waited for; matrix products, arithmetic and copies ran while one was open for 13% of the time, Pallas kernels for 0%

commit v1 on v0

v1 whole, which is shorter than its diff:
```python
import functools
import math

import jax
import jax.numpy as jnp
from jax import lax
from jax.experimental import pallas as pl
from jax.experimental.pallas import tpu as pltpu
from jax.sharding import PartitionSpec as P

HEAD_DIM = 72
SEQ = 256
LAYERS = 1


EPSILON = 1e-06
PRECISE = lax.Precision.HIGHEST
GELU_COEFF = math.sqrt(2.0 / math.pi)
CUBIC_COEFF = 0.044715


def time_features(timesteps, width):
    half_width = width // 2
    freq_rates = jnp.exp(
        -math.log(10000.0) * jnp.arange(half_width, dtype=jnp.float32) / half_width
    )
    angles = timesteps.astype(jnp.float32)[:, None] * freq_rates[None, :]
    return jnp.concatenate([jnp.cos(angles), jnp.sin(angles)], axis=1)


def layer_norm(values):
    average = jnp.mean(values, axis=-1, keepdims=True)
    centred = values - average
    inverse = lax.rsqrt(jnp.mean(centred * centred, axis=-1, keepdims=True) + EPSILON)
    return (centred * inverse, inverse)


def norm_back(normed, inverse, grad_normed):
    first = jnp.mean(grad_normed, axis=-1, keepdims=True)
    second = jnp.mean(grad_normed * normed, axis=-1, keepdims=True)
    return inverse * (grad_normed - first - normed * second)


def gelu_value(values):
    return (
        0.5
        * values
        * (1.0 + jnp.tanh(GELU_COEFF * (values + CUBIC_COEFF * values * values * values)))
    )


def gelu_slope(values):
    tangent = jnp.tanh(GELU_COEFF * (values + CUBIC_COEFF * values * values * values))
    return 0.5 * (1.0 + tangent) + 0.5 * values * (1.0 - tangent * tangent) * GELU_COEFF * (
        1.0 + 3.0 * CUBIC_COEFF * values * values
    )


def silu_slope(values):
    logistic = jax.nn.sigmoid(values)
    return logistic * (1.0 + values * (1.0 - logistic))


MESH = pl.DeviceIdType.MESH
ON_CHIP = pl.BlockSpec(memory_space=pltpu.VMEM)
IN_PLACE = pl.BlockSpec(memory_space=pl.ANY)
DMA = pltpu.SemaphoreType.DMA


def comm_call(body, out_shape, scratch, number, args, in_specs=None, out_specs=None):
    many = isinstance(out_shape, (list, tuple))
    return pl.pallas_call(
        body,
        out_shape=out_shape,
        in_specs=in_specs or [ON_CHIP] * len(args),
        out_specs=out_specs or ([ON_CHIP] * len(out_shape) if many else ON_CHIP),
        scratch_shapes=scratch,
        compiler_params=pltpu.CompilerParams(
            collective_id=number, has_side_effects=True, vmem_limit_bytes=48 * 1024 * 1024
        ),
    )(*args)


def greet(peers):
    barrier = pltpu.get_barrier_semaphore()
    for peer in peers:
        pl.semaphore_signal(barrier, inc=1, device_id=peer, device_id_type=MESH)
    pl.semaphore_wait(barrier, len(peers))


def push(source, target, send_sem, recv_sem, peer):
    copy = pltpu.make_async_remote_copy(
        src_ref=source,
        dst_ref=target,
        send_sem=send_sem,
        recv_sem=recv_sem,
        device_id=peer,
        device_id_type=MESH,
    )
    copy.start()
    return copy


def tensor_ring(tensor_count):
    group = lax.axis_index("dp")
    place = lax.axis_index("tensor")
    cores = 2 if tensor_count % 2 == 0 else 1
    chips = tensor_count // cores
    chip, core = place // cores, lax.rem(place, cores)
    return group, chip, core, chips, cores


def gather_rows_body(tensor_count, own_ref, out_ref, send_sem, recv_sem, local_sem):
    group, chip, core, chips, cores = tensor_ring(tensor_count)
    place = chip * cores + core
    far = [(group, lax.rem(chip + step, chips) * cores + core) for step in range(1, chips)]
    near = [(group, chip * cores + lax.rem(core + step, cores)) for step in range(1, cores)]
    greet(far + near)
    copies = []
    for index, peer in enumerate(far):
        copies.append(push(own_ref, out_ref.at[place], send_sem.at[index], recv_sem.at[index], peer))
    arrivals = list(copies)
    base = len(far)
    for peer in near:
        copies.append(push(own_ref, out_ref.at[place], send_sem.at[base], recv_sem.at[base], peer))
        base += 1
    keep = pltpu.make_async_copy(own_ref, out_ref.at[place], local_sem)
    keep.start()
    for step in range(1, chips):
        arrivals[step - 1].wait_recv()
        block = lax.rem(chip + chips - step, chips) * cores + core
        for peer in near:
            copies.append(
                push(out_ref.at[block], out_ref.at[block], send_sem.at[base], recv_sem.at[base], peer)
            )
            base += 1
    for copy in copies[len(far) :]:
        copy.wait_recv()
    for copy in copies:
        copy.wait_send()
    keep.wait()


def gather_rows(values, number):
    tensor_count = lax.axis_size("tensor")
    rows, cols = values.shape
    gathered = comm_call(
        functools.partial(gather_rows_body, tensor_count),
        jax.ShapeDtypeStruct((tensor_count, rows, cols), values.dtype),
        [DMA((2 * tensor_count,)), DMA((2 * tensor_count,)), DMA],
        number,
        (values,),
    )
    return gathered.reshape(tensor_count * rows, cols)


def scatter_rows_body(
    tensor_count, terms_ref, out_ref, near_ref, sum_ref, far_ref, send_sem, recv_sem
):
    group, chip, core, chips, cores = tensor_ring(tensor_count)
    far = [(group, lax.rem(chip + step, chips) * cores + core) for step in range(1, chips)]
    near = [lax.rem(core + step, cores) for step in range(1, cores)]
    greet(far + [(group, chip * cores + other) for other in near])
    copies = []
    base = 0
    arrivals = []
    for step in list(range(1, chips)) + [0]:
        column = []
        target_chip = lax.rem(chip + step, chips)
        for slot, other in enumerate(near):
            copy = push(
                terms_ref.at[target_chip * cores + other],
                near_ref.at[step, slot],
                send_sem.at[base],
                recv_sem.at[base],
                (group, chip * cores + other),
            )
            base += 1
            column.append(copy)
            copies.append(copy)
        arrivals.append((step, target_chip, column))
    sent_far = []
    for step, target_chip, column in arrivals:
        total = terms_ref[target_chip * cores + core].astype(jnp.float32)
        for slot, copy in enumerate(column):
            copy.wait_recv()
            total = total + near_ref[step, slot].astype(jnp.float32)
        if step:
            sum_ref[step - 1] = total.astype(jnp.bfloat16)
            copy = push(
                sum_ref.at[step - 1],
                far_ref.at[step - 1],
                send_sem.at[base],
                recv_sem.at[base],
                far[step - 1],
            )
            base += 1
            sent_far.append(copy)
            copies.append(copy)
        else:
            out_ref[...] = total
    for slot, copy in enumerate(sent_far):
        copy.wait_recv()
        out_ref[...] += far_ref[slot].astype(jnp.float32)
    for copy in copies:
        copy.wait_send()


def scatter_rows(values, number):
    tensor_count = lax.axis_size("tensor")
    cols = values.shape[1]
    rows = values.shape[0] // tensor_count
    cores = 2 if tensor_count % 2 == 0 else 1
    chips = tensor_count // cores
    return comm_call(
        functools.partial(scatter_rows_body, tensor_count),
        jax.ShapeDtypeStruct((rows, cols), jnp.float32),
        [
            pltpu.VMEM((chips, max(cores - 1, 1), rows, cols), jnp.bfloat16),
            pltpu.VMEM((max(chips - 1, 1), rows, cols), jnp.bfloat16),
            pltpu.VMEM((max(chips - 1, 1), rows, cols), jnp.bfloat16),
            DMA((2 * tensor_count,)),
            DMA((2 * tensor_count,)),
        ],
        number,
        (values.reshape(tensor_count, rows, cols),),
    )


def axis_peers(group_count, tensor_count):
    group, place = lax.axis_index("dp"), lax.axis_index("tensor")
    others = [(lax.rem(group + step, group_count), place) for step in range(1, group_count)]
    mates = [(group, lax.rem(place + step, tensor_count)) for step in range(1, tensor_count)]
    return group, place, others, mates


def modulation_body(
    group_count, tensor_count, terms_ref, out_ref, landed_ref, send_sem, recv_sem, send_two, recv_two
):
    group, place, others, mates = axis_peers(group_count, tensor_count)
    greet(others + mates)
    copies = []
    for index, peer in enumerate(others):
        copies.append(
            push(
                terms_ref.at[peer[0]],
                landed_ref.at[index],
                send_sem.at[index],
                recv_sem.at[index],
                peer,
            )
        )
    total = terms_ref[group]
    for index, copy in enumerate(copies):
        copy.wait_recv()
        total = total + landed_ref[index]
    out_ref[place] = total
    spread = []
    for index, peer in enumerate(mates):
        spread.append(
            push(out_ref.at[place], out_ref.at[place], send_two.at[index], recv_two.at[index], peer)
        )
    for copy in spread:
        copy.wait_recv()
    for copy in copies + spread:
        copy.wait_send()


def sum_modulation(terms, number):
    group_count, tensor_count = lax.axis_size("dp"), lax.axis_size("tensor")
    _, latents, cols = terms.shape
    return comm_call(
        functools.partial(modulation_body, group_count, tensor_count),
        jax.ShapeDtypeStruct((tensor_count, latents, cols), jnp.float32),
        [
            pltpu.VMEM((max(group_count - 1, 1), latents, cols), jnp.float32),
            DMA((group_count,)),
            DMA((group_count,)),
            DMA((tensor_count,)),
            DMA((tensor_count,)),
        ],
        number,
        (terms,),
    )


def collect_body(
    group_count,
    tensor_count,
    split_ref,
    own_ref,
    split_out,
    own_out,
    landed_ref,
    send_sem,
    recv_sem,
    send_two,
    recv_two,
):
    group, place, others, mates = axis_peers(group_count, tensor_count)
    greet(others + mates)
    copies = []
    for index, peer in enumerate(others):
        copies.append(
            push(own_ref, own_out.at[group], send_two.at[index], recv_two.at[index], peer)
        )
    first = []
    for index, peer in enumerate(mates):
        first.append(
            push(
                split_ref.at[peer[1]],
                landed_ref.at[index],
                send_sem.at[index],
                recv_sem.at[index],
                peer,
            )
        )
    own_out[group] = own_ref[...]
    total = split_ref[place]
    for index, copy in enumerate(first):
        copy.wait_recv()
        total = total + landed_ref[index]
    split_out[group] = total
    count = len(others)
    for index, peer in enumerate(others):
        copies.append(
            push(
                split_out.at[group],
                split_out.at[group],
                send_two.at[count + index],
                recv_two.at[count + index],
                peer,
            )
        )
    for copy in copies:
        copy.wait_recv()
    for copy in copies + first:
        copy.wait_send()


def collect(split, own, number):
    group_count, tensor_count = lax.axis_size("dp"), lax.axis_size("tensor")
    wide, narrow = split.shape[2], own.shape[1]
    return comm_call(
        functools.partial(collect_body, group_count, tensor_count),
        [
            jax.ShapeDtypeStruct((group_count, 1, wide), jnp.float32),
            jax.ShapeDtypeStruct((group_count, 1, narrow), jnp.float32),
        ],
        [
            pltpu.VMEM((max(tensor_count - 1, 1), 1, wide), jnp.float32),
            DMA((tensor_count,)),
            DMA((tensor_count,)),
            DMA((2 * group_count,)),
            DMA((2 * group_count,)),
        ],
        number,
        (split, own),
    )


def spread_body(group_count, tensor_count, one_ref, two_ref, one_out, two_out, send_sem, recv_sem):
    group, place, others, mates = axis_peers(group_count, tensor_count)
    greet(mates)
    copies = []
    count = len(mates)
    for index, peer in enumerate(mates):
        copies.append(
            push(one_ref, one_out.at[place], send_sem.at[index], recv_sem.at[index], peer)
        )
        copies.append(
            push(
                two_ref,
                two_out.at[place],
                send_sem.at[count + index],
                recv_sem.at[count + index],
                peer,
            )
        )
    one_out[place] = one_ref[...]
    two_out[place] = two_ref[...]
    for copy in copies:
        copy.wait_recv()
    for copy in copies:
        copy.wait_send()


def spread_pair(one, two, number):
    group_count, tensor_count = lax.axis_size("dp"), lax.axis_size("tensor")
    return comm_call(
        functools.partial(spread_body, group_count, tensor_count),
        [
            jax.ShapeDtypeStruct((tensor_count,) + one.shape, jnp.float32),
            jax.ShapeDtypeStruct((tensor_count,) + two.shape, jnp.float32),
        ],
        [DMA((2 * tensor_count,)), DMA((2 * tensor_count,))],
        number,
        (one, two),
    )


def gather_weight(weight):
    return lax.all_gather(weight, "dp", axis=0, tiled=True)


def scatter_weight(grad):
    return lax.psum_scatter(
        grad.astype(jnp.bfloat16), "dp", scatter_dimension=0, tiled=True
    ).astype(jnp.float32)


def dot_low(left, right, left_dim, right_dim):
    return lax.dot_general(
        left, right, (((left_dim,), (right_dim,)), ((), ())), preferred_element_type=jnp.float32
    )


def split_heads(values, latent_count):
    return values.reshape(latent_count, SEQ, -1, HEAD_DIM)


def local(
    tokens,
    timesteps,
    labels,
    time_weight,
    class_table,
    mod_weight,
    mod_bias,
    qkv_weight,
    qv_bias,
    proj_weight,
    proj_bias,
    up_weight,
    up_bias,
    down_weight,
    down_bias,
    grad_output,
):
    rows_own, model_width = tokens.shape
    tensor_count = lax.axis_size("tensor")
    group_count = lax.axis_size("dp")
    tensor_place = lax.axis_index("tensor")
    group_rows = rows_own * tensor_count
    latent_count = group_rows // SEQ
    head_cols = qkv_weight.shape[3]
    unit_cols = up_weight.shape[2]
    mod_cols = mod_weight.shape[2]
    own_rows = qkv_weight.shape[2]
    head_start = tensor_place * head_cols
    unit_start = tensor_place * unit_cols
    score_scale = 1.0 / math.sqrt(HEAD_DIM)

    attn_own = jnp.concatenate(
        [qkv_weight[0, 0], qkv_weight[0, 1], qkv_weight[0, 2], proj_weight[0].T], axis=1
    )
    attn_full = gather_weight(attn_own)
    up_full = gather_weight(up_weight[0])
    down_full = gather_weight(down_weight[0].T)
    qkv_full = attn_full[:, : 3 * head_cols]
    proj_full = attn_full[:, 3 * head_cols :]

    features = time_features(timesteps, time_weight.shape[0])
    one_hot = (
        labels[:, None] == jnp.arange(class_table.shape[0], dtype=jnp.int32)[None, :]
    ).astype(jnp.float32)
    condition = jnp.dot(features, time_weight, precision=PRECISE) + jnp.dot(
        one_hot, class_table, precision=PRECISE
    )
    cond_act = jax.nn.silu(condition).astype(jnp.bfloat16)
    mod_terms = jnp.dot(cond_act, mod_weight[0], preferred_element_type=jnp.float32)
    mod_sum = sum_modulation(mod_terms.reshape(group_count, latent_count, mod_cols), 1)
    modulation = mod_sum.transpose(1, 0, 2).reshape(latent_count, -1) + mod_bias

    if SEQ % rows_own == 0:
        my_latent = (tensor_place * rows_own) // SEQ
        rows_mod = lax.dynamic_slice_in_dim(modulation, my_latent, 1, 0)
        mine = (jnp.arange(latent_count, dtype=jnp.int32) == my_latent)[:, None]

        def per_latent(values):
            return jnp.where(mine, jnp.sum(values, axis=0)[None, :], 0.0)

    else:
        row_latent = (tensor_place * rows_own + jnp.arange(rows_own, dtype=jnp.int32)) // SEQ
        selector = (
            row_latent[:, None] == jnp.arange(latent_count, dtype=jnp.int32)[None, :]
        ).astype(jnp.float32)
        rows_mod = jnp.dot(selector, modulation, precision=PRECISE)

        def per_latent(values):
            return jnp.dot(selector.T, values, precision=PRECISE)

    shift_attn, scale_attn, gate_attn, shift_mlp, scale_mlp, gate_mlp = [
        rows_mod[:, segment * model_width : (segment + 1) * model_width] for segment in range(6)
    ]

    def attention_scores(queries, key_rows):
        return (
            jnp.einsum(
                "bqhd,bkhd->bhqk",
                split_heads(queries, latent_count),
                split_heads(key_rows, latent_count),
                preferred_element_type=jnp.float32,
            )
            * score_scale
        )

    bias_query = lax.dynamic_slice_in_dim(qv_bias[0, 0], head_start, head_cols, 0)
    bias_value = lax.dynamic_slice_in_dim(qv_bias[0, 1], head_start, head_cols, 0)
    unit_bias = lax.dynamic_slice_in_dim(up_bias[0], unit_start, unit_cols, 0)
    bias_qkv = jnp.concatenate([bias_query, jnp.zeros_like(bias_query), bias_value])

    normed_attn, inverse_attn = layer_norm(tokens)
    attn_in = gather_rows((normed_attn * (1.0 + scale_attn) + shift_attn).astype(jnp.bfloat16), 2)
    qkv_rows = (dot_low(attn_in, qkv_full, 1, 0) + bias_qkv).astype(jnp.bfloat16)
    queries = qkv_rows[:, :head_cols]
    key_rows = qkv_rows[:, head_cols : 2 * head_cols]
    value_rows = qkv_rows[:, 2 * head_cols :]
    scores = attention_scores(queries, key_rows)
    log_total = jnp.log(jnp.sum(jnp.exp(scores), axis=-1, keepdims=True))
    prob_full = jnp.exp(scores - log_total)
    prob_low = prob_full.astype(jnp.bfloat16)
    attended = (
        jnp.einsum(
            "bhqk,bkhd->bqhd",
            prob_low,
            split_heads(value_rows, latent_count),
            preferred_element_type=jnp.float32,
        )
        .astype(jnp.bfloat16)
        .reshape(group_rows, head_cols)
    )
    attn_out = (
        scatter_rows(dot_low(attended, proj_full, 1, 1).astype(jnp.bfloat16), 3) + proj_bias[0]
    )
    middle = tokens + gate_attn * attn_out
    normed_mlp, inverse_mlp = layer_norm(middle)
    mlp_in = gather_rows((normed_mlp * (1.0 + scale_mlp) + shift_mlp).astype(jnp.bfloat16), 4)
    pre_act = dot_low(mlp_in, up_full, 1, 0) + unit_bias
    gelu_low = gelu_value(pre_act).astype(jnp.bfloat16)
    mlp_out = (
        scatter_rows(dot_low(gelu_low, down_full, 1, 1).astype(jnp.bfloat16), 5) + down_bias[0]
    )
    output = middle + gate_mlp * mlp_out

    d_mlp = grad_output * gate_mlp
    d_gate_mlp = per_latent(grad_output * mlp_out)
    down_bias_part = jnp.sum(d_mlp, axis=0)
    d_mlp_all = gather_rows(d_mlp.astype(jnp.bfloat16), 6)
    grad_down = scatter_weight(dot_low(d_mlp_all, gelu_low, 0, 0))
    d_gelu = dot_low(d_mlp_all, down_full, 1, 0)
    d_pre = d_gelu * gelu_slope(pre_act)
    unit_part = jnp.sum(d_pre, axis=0)
    d_pre_low = d_pre.astype(jnp.bfloat16)
    grad_up = scatter_weight(dot_low(mlp_in, d_pre_low, 0, 0))
    d_mlp_in = scatter_rows(dot_low(d_pre_low, up_full, 1, 1).astype(jnp.bfloat16), 7)
    d_shift_mlp = per_latent(d_mlp_in)
    d_scale_mlp = per_latent(d_mlp_in * normed_mlp)
    d_middle = grad_output + norm_back(normed_mlp, inverse_mlp, d_mlp_in * (1.0 + scale_mlp))
    d_attn = d_middle * gate_attn
    d_gate_attn = per_latent(d_middle * attn_out)
    proj_bias_part = jnp.sum(d_attn, axis=0)
    d_attn_all = gather_rows(d_attn.astype(jnp.bfloat16), 8)
    d_attended = dot_low(d_attn_all, proj_full, 1, 0).astype(jnp.bfloat16)
    d_heads = split_heads(d_attended, latent_count)
    grad_value = jnp.einsum(
        "bhqk,bqhd->bkhd", prob_low, d_heads, preferred_element_type=jnp.float32
    ).reshape(group_rows, head_cols)
    d_prob = jnp.einsum(
        "bqhd,bkhd->bhqk",
        d_heads,
        split_heads(value_rows, latent_count),
        preferred_element_type=jnp.float32,
    )
    row_delta = jnp.einsum(
        "bqhd,bqhd->bhq",
        d_heads,
        split_heads(attended, latent_count),
        preferred_element_type=jnp.float32,
    )
    d_score_low = (prob_full * (d_prob - row_delta[..., None])).astype(jnp.bfloat16)
    grad_query = (
        jnp.einsum(
            "bhqk,bkhd->bqhd",
            d_score_low,
            split_heads(key_rows, latent_count),
            preferred_element_type=jnp.float32,
        ).reshape(group_rows, head_cols)
        * score_scale
    )
    grad_key = (
        jnp.einsum(
            "bhqk,bqhd->bkhd",
            d_score_low,
            split_heads(queries, latent_count),
            preferred_element_type=jnp.float32,
        ).reshape(group_rows, head_cols)
        * score_scale
    )
    qv_part = jnp.concatenate([jnp.sum(grad_query, axis=0), jnp.sum(grad_value, axis=0)])
    low_rows = jnp.concatenate(
        [
            grad_query.astype(jnp.bfloat16),
            grad_key.astype(jnp.bfloat16),
            grad_value.astype(jnp.bfloat16),
        ],
        axis=1,
    )
    grad_attn = scatter_weight(
        jnp.concatenate(
            [dot_low(attn_in, low_rows, 0, 0), dot_low(d_attn_all, attended, 0, 0)], axis=1
        )
    )
    d_attn_in = scatter_rows(dot_low(low_rows, qkv_full, 1, 1).astype(jnp.bfloat16), 9)
    d_shift_attn = per_latent(d_attn_in)
    d_scale_attn = per_latent(d_attn_in * normed_attn)
    grad_tokens = d_middle + norm_back(normed_attn, inverse_attn, d_attn_in * (1.0 + scale_attn))

    d_mod_part = jnp.concatenate(
        [d_shift_attn, d_scale_attn, d_gate_attn, d_shift_mlp, d_scale_mlp, d_gate_mlp], axis=1
    )
    bias_cols = model_width // tensor_count
    split = jnp.concatenate(
        [
            d_mod_part[latent].reshape(tensor_count, 1, mod_cols)
            for latent in range(latent_count)
        ]
        + [
            proj_bias_part.reshape(tensor_count, 1, bias_cols),
            down_bias_part.reshape(tensor_count, 1, bias_cols),
        ],
        axis=2,
    )
    own = jnp.concatenate([unit_part, qv_part])[None, :]
    split_all, own_all = collect(split, own, 10)
    mod_end = latent_count * mod_cols
    d_mod_all = split_all[:, 0, :mod_end].reshape(group_count * latent_count, mod_cols)
    totals = jnp.concatenate(
        [
            jnp.sum(d_mod_all, axis=0),
            jnp.sum(split_all[:, 0, mod_end:], axis=0),
            jnp.sum(own_all[:, 0], axis=0),
        ]
    )[None, :]
    cond_wide = cond_act.astype(jnp.float32)
    grad_mod_weight = jnp.dot(cond_wide.T, d_mod_all, precision=PRECISE)[None]
    cond_back = jnp.dot(d_mod_all, mod_weight[0].astype(jnp.float32).T, precision=PRECISE)
    cond_parts, total_parts = spread_pair(cond_back, totals, 11)
    total_parts = total_parts[:, 0]
    ends = [mod_cols, bias_cols, bias_cols, unit_cols, head_cols, head_cols]
    pieces = []
    start = 0
    for width in ends:
        pieces.append(total_parts[:, start : start + width].reshape(1, -1))
        start += width
    modb_total, proj_total, down_total, unit_total, query_total, value_total = pieces
    d_condition = jnp.sum(cond_parts, axis=0) * silu_slope(condition)
    grad_time_weight = jnp.dot(features.T, d_condition, precision=PRECISE)
    grad_class_table = jnp.dot(one_hot.T, d_condition, precision=PRECISE)
    grad_qkv = grad_attn[:, : 3 * head_cols].reshape(own_rows, 3, head_cols).transpose(1, 0, 2)
    return (
        output,
        grad_tokens,
        grad_time_weight,
        grad_class_table,
        grad_mod_weight,
        modb_total,
        grad_qkv[None],
        jnp.concatenate([query_total, value_total])[None],
        grad_attn[:, 3 * head_cols :].T[None],
        proj_total,
        grad_up[None],
        unit_total,
        grad_down.T[None],
        down_total,
    )


def solution(mesh):
    in_specs = (
        P(("dp", "tensor"), None),
        P(),
        P(),
        P(None, "dp"),
        P(None, "dp"),
        P(None, "dp", "tensor"),
        P(),
        P(None, None, "dp", "tensor"),
        P(),
        P(None, "tensor", "dp"),
        P(),
        P(None, "dp", "tensor"),
        P(),
        P(None, "tensor", "dp"),
        P(),
        P(("dp", "tensor"), None),
    )
    out_specs = (
        P(("dp", "tensor"), None),
        P(("dp", "tensor"), None),
        P(None, "dp"),
        P(None, "dp"),
        P(None, "dp", "tensor"),
        P(),
        P(None, None, "dp", "tensor"),
        P(),
        P(None, "tensor", "dp"),
        P(),
        P(None, "dp", "tensor"),
        P(),
        P(None, "tensor", "dp"),
        P(),
    )
    return jax.shard_map(local, mesh=mesh, in_specs=in_specs, out_specs=out_specs, check_vma=False)
```

time: 838 us -> 492 us (0.59)
  waiting for transfers between devices: 506 us -> 264 us
  blocking collectives: 152 us -> 0 us
  Pallas kernels: 0 us -> 112 us
  matrix products: 82.3 us -> 56 us
  local copies, waits for them, and re-layouts: 39.9 us -> 24.6 us
  other arithmetic: 32.1 us -> 17.7 us
    reduce_scatter x7 -> x2, waiting for transfers between devices: 255 us -> 142 us  [scatter_weight(): lax.psum_scatter(grad.astype(jnp.bfloat16), 'dp', scatter_dimension=0, ti...]
    pallas_call x0 -> x11, Pallas kernels: none -> 112 us  [comm_call(): pl.pallas_call(body, out_shape=out_shape, in_specs=in_specs or [ON_CHIP]...]
    all_gather x3 -> x0, blocking collectives: 89.9 us -> none  [the longest x1 35.3 us: gather_layer(): lax.all_gather(proj_weight[current], 'dp', axis=1, tiled=True)]
    all_gather x7 -> x3, waiting for transfers between devices: 179 us -> 99.7 us  [gather_weight(): return lax.all_gather(weight, 'dp', axis=0, tiled=True)]
    psum x3 -> x0, blocking collectives: 62 us -> none  [the longest x1 40.3 us: local(): lax.psum((jnp.stack(qv_bias_list), jnp.stack(proj_bias_list), jnp.stack(u...]
    unnamed x18 -> x7, waiting for transfers between devices: 71.8 us -> 22.5 us
    dot_general x27 -> x14, matrix products: 61.5 us -> 38.2 us  [the longest x12 36.2 us: dot_low(): lax.dot_general(left, right, (((left_dim,), (right_dim,)), ((), ())), pre...]
    unnamed x120 -> x176, local copies, waits for them, and re-layouts: 26.8 us -> 11.6 us
  transfers between devices with their start and end apart: 16 -> 6, of which waited for: 14 -> 6; matrix products, arithmetic and copies ran while one was open for 13% -> 10% of each run, Pallas kernels for 0% -> 14%
where the time goes in v1:
time: 492 us; the launch traced here: 491 us
  waiting for transfers between devices  264 us (54%)
  Pallas kernels  112 us (23%)
  matrix products  56 us (11%)
  local copies, waits for them, and re-layouts  24.6 us (5%)
  other arithmetic  17.7 us (4%)
  between operations  15.6 us (3%)
    reduce_scatter x2, waiting for transfers between devices, scatter_weight(): lax.psum_scatter(grad.astype(jnp.bfloat16), 'dp', scatter_dimension=0, ti...  142 us
    pallas_call x11, Pallas kernels, comm_call(): pl.pallas_call(body, out_shape=out_shape, in_specs=in_specs or [ON_CHIP]...  112 us
    all_gather x3, waiting for transfers between devices, gather_weight(): return lax.all_gather(weight, 'dp', axis=0, tiled=True)  99.7 us
    dot_general x12, matrix products, dot_low(): lax.dot_general(left, right, (((left_dim,), (right_dim,)), ((), ())), pre...  36.2 us
    unnamed x7, waiting for transfers between devices  22.5 us
    unnamed x176, local copies, waits for them, and re-layouts  11.6 us
  transfers between devices with their start and end apart: 6, of which 6 were waited for; matrix products, arithmetic and copies ran while one was open for 10% of the time, Pallas kernels for 14%

profile of v1, /device:TPU:0, one launch (start us, length us, event | category | flops | bytes accessed | tf_op | source)
XLA Modules:
  0.0 491.1 jit_solution(9464739130975019733)
XLA Ops:
  13.1 12.5 %shard_map.263 = f32[4,2,1728]{2,1,0:T(2,128)S(1)} custom-call(f32[8,2,1728]{2,1,0:T(2,128)S(1)} %copy.70.terms_ref), custom_call_target="tpu_custom_call" | custom-call | tf_op jit(solution)/shard_map/pallas_call | solution.py:72
  26.6 10.7 %shard_map.264 = bf16[4,128,1152]{2,1,0:T(8,128)(2,1)S(1)} custom-call(bf16[128,1152]{1,0:T(8,128)(2,1)S(1)} %add_convert_fusion.2.own_ref), custom_call_target="tpu_custom_call" | custom-call | tf_op jit(solution)/shard_map/pallas_call | solution.py:72
  39.6 29.0 %all-gather.5.cloned.1.call-done = bf16[1152,1152]{1,0:T(8,128)(2,1)} async-done(((bf16[144,1152]{1,0:T(8,128)(2,1)}), bf16[1152,1152]{1,0:T(8,128)(2,1)}) %all-gather.5.cloned.1.call-update) | async-done | bytes 2654224 | tf_op jit(solution)/shard_map/all_gather | solution.py:403
  68.6 2.9 add_convert_fusion
  73.8 3.2 convolution_convert_fusion.9
  77.4 2.4 convolution_convert_fusion.6
  79.8 11.1 %shard_map.265 = f32[128,1152]{1,0:T(8,128)S(1)} custom-call(bf16[4,128,1152]{2,1,0:T(8,128)(2,1)S(1)} %bitcast.133), custom_call_target="tpu_custom_call" | custom-call | tf_op jit(solution)/shard_map/pallas_call | solution.py:72
  91.9 10.4 %shard_map.266 = bf16[4,128,1152]{2,1,0:T(8,128)(2,1)S(1)} custom-call(bf16[128,1152]{1,0:T(8,128)(2,1)S(1)} %get-tuple-element.114.own_ref), custom_call_target="tpu_custom_call" | custom-call | tf_op jit(solution)/shard_map/pallas_call | solution.py:72
  102.4 2.0 fusion.8
  104.4 20.0 %all-gather.9.cloned.1.call-done = bf16[1,1152,1152]{2,1,0:T(8,128)(2,1)} async-done(((bf16[1,144,1152]{2,1,0:T(8,128)(2,1)}), bf16[1,1152,1152]{2,1,0:T(8,128)(2,1)}) %all-gather.9.cloned.1.call-update) | async-done | bytes 2654224 | tf_op jit(solution)/shard_map/all_gather | solution.py:403
  124.3 5.0 %convolution_add_fusion = f32[512,1152]{1,0:T(8,128)} fusion(bf16[512,1152]{1,0:T(8,128)(2,1)S(1)} %bitcast.129, bf16[1,1152,1152]{2,1,0:T(8,128)(2,1)} %all-gather.9.cloned.1.call-done, f32[1152]{0:T(1024)S(1)} %copy-done.57), kind=kOutput, calls=%fused_computation.7 | convolution fusion | flops 1359544320 | bytes 6197760 | tf_op jit(solution)/shard_map/dot_general | solution.py:413
  129.4 50.7 %all-gather.7.cloned.1.call-done = bf16[1152,1152]{1,0:T(8,128)(2,1)} async-done(((bf16[144,1152]{1,0:T(8,128)(2,1)}), bf16[1152,1152]{1,0:T(8,128)(2,1)}) %all-gather.7.cloned.1.call-update) | async-done | bytes 2654224 | tf_op jit(solution)/shard_map/all_gather | solution.py:403
  180.1 4.8 convolution_convert_fusion.5
  184.9 11.1 %shard_map.267 = f32[128,1152]{1,0:T(8,128)S(1)} custom-call(bf16[4,128,1152]{2,1,0:T(8,128)(2,1)S(1)} %bitcast.134), custom_call_target="tpu_custom_call" | custom-call | tf_op jit(solution)/shard_map/pallas_call | solution.py:72
  196.0 10.3 %shard_map.268 = bf16[4,128,1152]{2,1,0:T(8,128)(2,1)S(1)} custom-call(bf16[128,1152]{1,0:T(8,128)(2,1)S(1)} %get-tuple-element.115.own_ref), custom_call_target="tpu_custom_call" | custom-call | tf_op jit(solution)/shard_map/pallas_call | solution.py:72
  206.3 3.1 fusion.73
  211.3 11.1 %shard_map.269 = f32[128,1152]{1,0:T(8,128)S(1)} custom-call(bf16[4,128,1152]{2,1,0:T(8,128)(2,1)S(1)} %bitcast.132), custom_call_target="tpu_custom_call" | custom-call | tf_op jit(solution)/shard_map/pallas_call | solution.py:72
  223.3 1.9 multiply_reduce_fusion.10
  225.3 10.1 %shard_map.270 = bf16[4,128,1152]{2,1,0:T(8,128)(2,1)S(1)} custom-call(bf16[128,1152]{1,0:T(8,128)(2,1)S(1)} %multiply_convert_fusion.2.own_ref), custom_call_target="tpu_custom_call" | custom-call | tf_op jit(solution)/shard_map/pallas_call | solution.py:72
  235.4 3.0 convolution_convert_fusion.8
  242.5 2.3 multiply_convert_fusion.1
  247.6 4.6 fusion.67
  258.9 5.2 %copy.102 = bf16[1152,1152]{1,0:T(8,128)(2,1)} copy(bf16[1152,1152]{0,1:T(8,128)(2,1)} %pad_maximum_fusion) | data formatting | bytes 5308416
  265.7 3.3 convolution_convert_fusion.1
  269.2 3.5 convolution_convert_fusion.3
  272.7 11.1 %shard_map.271 = f32[128,1152]{1,0:T(8,128)S(1)} custom-call(bf16[4,128,1152]{2,1,0:T(8,128)(2,1)S(1)} %bitcast.131), custom_call_target="tpu_custom_call" | custom-call | tf_op jit(solution)/shard_map/pallas_call | solution.py:72
  284.7 3.4 convolution_convert_fusion
  290.2 10.0 %shard_map.272 = (f32[8,1,4032]{2,1,0:T(1,128)S(1)}, f32[8,1,1728]{2,1,0:T(1,128)S(1)}) custom-call(f32[4,1,4032]{2,1,0:T(1,128)S(1)} %concatenate.36.split_ref, f32[1,1728]{1,0:T(1,128)S(1)} %broadcast_in_dim.130.own_ref), custom_call_target="tpu_custom_call" | custom-call | tf_op jit(solution)/shard_map/pallas_call | solution.py:72
  301.3 4.2 shard_map.273
  314.1 21.1 %reduce-scatter.10.cloned.1.call-done = bf16[144,1152]{1,0:T(8,128)(2,1)} async-done(((bf16[1152,1152]{1,0:T(8,128)(2,1)}), bf16[144,1152]{1,0:T(8,128)(2,1)}) %reduce-scatter.10.cloned.1.call-update) | async-done | bytes 331792
  338.6 70.3 %reduce-scatter.6.cloned.1.call-done = bf16[144,1152]{1,0:T(8,128)(2,1)} async-done(((bf16[1152,1152]{1,0:T(8,128)(2,1)}), bf16[144,1152]{1,0:T(8,128)(2,1)}) %reduce-scatter.6.cloned.1.call-update) | async-done | bytes 331792 | tf_op jit(solution)/shard_map/reduce_scatter | solution.py:407
  410.8 71.6 %reduce-scatter.8.cloned.1.call-done = bf16[144,1152]{1,0:T(8,128)(2,1)} async-done(((bf16[1152,1152]{1,0:T(8,128)(2,1)}), bf16[144,1152]{1,0:T(8,128)(2,1)}) %reduce-scatter.8.cloned.1.call-update) | async-done | bytes 331792 | tf_op jit(solution)/shard_map/reduce_scatter | solution.py:407
  (289 shorter events, 49.7 us)
Async XLA Ops:
  7.2 61.3 %all-gather.5.cloned.1.call-start = ((), (), s32[]{:S(2)}) async-start(), calls=%async_computation.3 | async-start | bytes 2985984 | tf_op jit(solution)/shard_map/all_gather | solution.py:403
  8.4 17.4 %copy-start.51 = (f32[1,6912]{1,0:T(1,128)S(1)}, f32[1,6912]{1,0:T(1,128)}, u32[]{:S(2)}) copy-start(f32[1,6912]{1,0:T(1,128)} %param.22) | copy-start | bytes 82948
  8.4 17.6 %copy-start.4 = (f32[128,1152]{1,0:T(8,128)S(1)}, f32[128,1152]{1,0:T(8,128)}, u32[]{:S(2)}) copy-start(f32[128,1152]{1,0:T(8,128)} %param.16) | copy-start | bytes 1769476
  10.4 114.0 %all-gather.9.cloned.1.call-start = ((), (), s32[]{:S(2)}) async-start(), calls=%async_computation.7 | async-start | bytes 2985984 | tf_op jit(solution)/shard_map/all_gather | solution.py:403
  11.1 169.0 %all-gather.7.cloned.1.call-start = ((), (), s32[]{:S(2)}) async-start(), calls=%async_computation.4 | async-start | bytes 2985984 | tf_op jit(solution)/shard_map/all_gather | solution.py:403
  11.9 323.3 %reduce-scatter.10.cloned.1.call-start = ((), (), s32[]{:S(2)}) async-start(), calls=%async_computation.8 | async-start | bytes 2985984
  13.1 24.2 %copy-start.63 = (f32[1,1152]{1,0:T(1,128)S(1)}, f32[1,1152]{1,0:T(1,128)}, u32[]{:S(2)}) copy-start(f32[1,1152]{1,0:T(1,128)} %param.26) | copy-start | bytes 13828
  13.1 24.2 %copy-start.64 = (f32[1,1152]{1,0:T(1,128)S(1)}, f32[1,1152]{1,0:T(1,128)}, u32[]{:S(2)}) copy-start(f32[1,1152]{1,0:T(1,128)} %param.30) | copy-start | bytes 13828
  13.1 24.9 %copy-start.54 = (f32[1,2,1152]{2,1,0:T(2,128)S(1)}, f32[1,2,1152]{2,1,0:T(2,128)}, u32[]{:S(2)}) copy-start(f32[1,2,1152]{2,1,0:T(2,128)} %param.24) | copy-start | bytes 27652
  26.0 45.5 %copy-start.26 = (f32[1152]{0:T(1024)}, f32[1152]{0:T(1024)S(1)}, u32[]{:S(2)}) copy-start(f32[1152]{0:T(1024)S(1)} %get-tuple-element.81) | copy-start | bytes 13828
  26.0 64.9 %copy-start.29 = (f32[1152]{0:T(1024)}, f32[1152]{0:T(1024)S(1)}, u32[]{:S(2)}) copy-start(f32[1152]{0:T(1024)S(1)} %get-tuple-element.82) | copy-start | bytes 13828
  26.0 65.3 %copy-start.31 = (f32[1152]{0:T(1024)}, f32[1152]{0:T(1024)S(1)}, u32[]{:S(2)}) copy-start(f32[1152]{0:T(1024)S(1)} %get-tuple-element.79) | copy-start | bytes 13828
  26.0 65.3 %copy-start.34 = (f32[1152]{0:T(1024)}, f32[1152]{0:T(1024)S(1)}, u32[]{:S(2)}) copy-start(f32[1152]{0:T(1024)S(1)} %get-tuple-element.78) | copy-start | bytes 13828
  37.3 53.6 %copy-start.36 = (f32[1152]{0:T(1024)}, f32[1152]{0:T(1024)S(1)}, u32[]{:S(2)}) copy-start(f32[1152]{0:T(1024)S(1)} %reduce.12) | copy-start | bytes 13828
  102.3 22.0 %copy-start.2 = (bf16[4,128,1152]{2,1,0:T(8,128)(2,1)}, bf16[4,128,1152]{2,1,0:T(8,128)(2,1)S(1)}, u32[]{:S(2)}) copy-start(bf16[4,128,1152]{2,1,0:T(8,128)(2,1)S(1)} %shard_map.266) | copy-start | bytes 3538948
  102.3 22.0 %copy-start.57 = (f32[1152]{0:T(1024)S(1)}, f32[1152]{0:T(1024)}, u32[]{:S(2)}) copy-start(f32[1152]{0:T(1024)} %dynamic-slice_reduce_fusion) | copy-start | bytes 13828
  180.1 26.2 %copy-start.78 = (f32[512,1152]{1,0:T(8,128)S(1)}, f32[512,1152]{1,0:T(8,128)}, u32[]{:S(2)}) copy-start(f32[512,1152]{1,0:T(8,128)} %convolution_add_fusion) | copy-start | bytes 7077892
  184.9 21.4 %copy-start.76 = (bf16[1152,1152]{1,0:T(8,128)(2,1)S(1)}, bf16[1152,1152]{1,0:T(8,128)(2,1)}, u32[]{:S(2)}) copy-start(bf16[1152,1152]{1,0:T(8,128)(2,1)} %all-gather.7.cloned.1.call-done) | copy-start | bytes 7962628
  264.1 144.9 %reduce-scatter.6.cloned.1.call-start = ((), (), s32[]{:S(2)}) async-start(), calls=%async_computation.5 | async-start | bytes 2985984 | tf_op jit(solution)/shard_map/reduce_scatter | solution.py:407
  269.1 213.4 %reduce-scatter.8.cloned.1.call-start = ((), (), s32[]{:S(2)}) async-start(), calls=%async_computation.6 | async-start | bytes 2985984 | tf_op jit(solution)/shard_map/reduce_scatter | solution.py:407
  269.1 15.5 %copy-start.52 = (pred[2]{0:T(512)(128)(4,1)}, pred[2]{0:T(512)(128)(4,1)S(1)}, u32[]{:S(2)}) copy-start(pred[2]{0:T(512)(128)(4,1)S(1)} %iota_compare_fusion.3) | copy-start | bytes 10
  288.2 20.4 %copy-start.39 = (bf16[16,144]{1,0:T(8,128)(2,1)S(1)}, bf16[16,144]{1,0:T(8,128)(2,1)}, u32[]{:S(2)}) copy-start(bf16[16,144]{1,0:T(8,128)(2,1)} %copy-done.38) | copy-start | bytes 13828
  288.2 21.9 %copy-start.74 = (f32[128]{0:T(128)S(1)}, f32[128]{0:T(128)}, u32[]{:S(2)}) copy-start(f32[128]{0:T(128)} %get-tuple-element.67) | copy-start | bytes 1540
  288.2 21.9 %copy-start.73 = (f32[128]{0:T(128)S(1)}, f32[128]{0:T(128)}, u32[]{:S(2)}) copy-start(f32[128]{0:T(128)} %get-tuple-element.68) | copy-start | bytes 1540
  288.3 22.5 %copy-start.41 = (f32[16,128]{1,0:T(8,128)S(1)}, f32[16,128]{1,0:T(8,128)}, u32[]{:S(2)}) copy-start(f32[16,128]{1,0:T(8,128)} %copy-done.40) | copy-start | bytes 24580
  288.3 22.5 %copy-start.43 = (f32[16,128]{1,0:T(8,128)S(1)}, f32[16,128]{1,0:T(8,128)}, u32[]{:S(2)}) copy-start(f32[16,128]{1,0:T(8,128)} %copy-done.42) | copy-start | bytes 24580
  288.3 23.5 %copy-start.72 = (s32[16]{0:T(128)S(1)}, s32[16]{0:T(128)}, u32[]{:S(2)}) copy-start(s32[16]{0:T(128)} %param.18) | copy-start | bytes 196
  289.5 23.6 %copy-start.10 = (f32[128,1152]{1,0:T(8,128)S(1)}, f32[128,1152]{1,0:T(8,128)}, u32[]{:S(2)}) copy-start(f32[128,1152]{1,0:T(8,128)} %copy-done.9) | copy-start | bytes 1769476
  289.5 23.6 %copy-start.28 = (f32[1152]{0:T(1024)S(1)}, f32[1152]{0:T(1024)}, u32[]{:S(2)}) copy-start(f32[1152]{0:T(1024)} %copy-done.26) | copy-start | bytes 13828
  289.5 23.6 %copy-start.60 = (f32[128]{0:T(128)S(1)}, f32[128]{0:T(128)}, u32[]{:S(2)}) copy-start(f32[128]{0:T(128)} %copy-done.58) | copy-start | bytes 1540
  289.5 23.6 %copy-start.67 = (f32[128]{0:T(128)S(1)}, f32[128]{0:T(128)}, u32[]{:S(2)}) copy-start(f32[128]{0:T(128)} %copy-done.65) | copy-start | bytes 1540
  336.6 147.7 %copy-start.1 = (f32[1001,144]{0,1:T(8,128)S(1)}, f32[1001,144]{0,1:T(8,128)}, u32[]{:S(2)}) copy-start(f32[1001,144]{0,1:T(8,128)} %param.20) | copy-start | bytes 1729732
  (56 other events, 391.7 us)
Sparse Core Ops, SparseCore 0:
  10.8 57.7 all-gather.4
  70.8 53.5 all-gather.8
  126.5 53.5 all-gather.6
  264.2 70.9 reduce-scatter.9
  338.7 70.2 reduce-scatter.5
  412.5 69.8 reduce-scatter.7
